TPU v7x, 32 devices: a whole 2x2x4 slice. The times are simulated.
32 devices in a mesh: groups: 1, blk: 16 (over z, y, x), heads: 2 (over core).
Axes of the slice: x: 2, y: 2, z: 4, core: 2. Of those that a mesh axis runs over, the one named last changes fastest.
Arguments:
- queries: bfloat16 [4096, 2048], P(('groups', 'blk', 'heads')), may hold values from -186 to 186
- keys: bfloat16 [4096, 1024], P(('groups', 'blk', 'heads')), may hold values from -6 to 6
- values: bfloat16 [4096, 1024], P(('groups', 'blk', 'heads')), may hold values from -6 to 6
- upstream: bfloat16 [4096, 2048], P(('groups', 'blk', 'heads')), may hold values from -6 to 6
- doc_ids: int32 [32], P('groups'), may hold values from 0 to 3, never falling along the last dimension, each value on 1 to 16 neighbouring positions
- band: int32 [32], P('groups'), may hold values from 0 to 8, as said below
Outputs:
- query_grad: bfloat16 [4096, 2048], P(('groups', 'blk', 'heads'))
- key_gradient: bfloat16 [4096, 1024], P(('groups', 'blk', 'heads'))
- value_gradient: bfloat16 [4096, 1024], P(('groups', 'blk', 'heads'))
Inputs may be any that keep to these rules, and one draw needn't show every extreme that they name: `band`: earlier blocks a query block may see; some block sees 8 and some sees 0.
All inputs are finite; a program needn't handle non-finite values.
Results may differ from a plain program's by a relative error of at most 0.0083.
Values may be sent and summed in bfloat16 or wider, within the bound.
A program may use at most 64 MiB of HBM per device.

v0:
```python
import functools
import math

import jax
import jax.numpy as jnp
from jax import lax
from jax.experimental import pallas as pl
from jax.experimental.pallas import tpu as pltpu
from jax.sharding import PartitionSpec as P

HEAD = 128
SCALE = 168 ** -0.5
LOG2E = math.log2(math.e)
WINDOW = 1024
BLOCK = 128
WB = WINDOW // BLOCK
GROUP = 2
QW = GROUP * HEAD
MESH = pl.DeviceIdType.MESH
HIDDEN = -1e30
SPAN = WINDOW + BLOCK
NT = (((1,), (1,)), ((), ()))
TN = (((0,), (0,)), ((), ()))


def place(cores):
    chips = WB // cores
    blk, core = lax.axis_index("blk"), lax.axis_index("heads")
    return blk // chips, (blk % chips) * cores + core


def device_of(cores, plane, local):
    return {"blk": plane * (WB // cores) + local // cores, "heads": local % cores}


def greet(cores, planes, plane, me):
    barrier = pltpu.get_barrier_semaphore()

    def signal(where):
        pl.semaphore_signal(barrier, inc=1, device_id=where, device_id_type=MESH)

    for r in range(1, WB):
        signal(device_of(cores, plane, (me + r) % WB))

    @pl.when(plane > 0)
    def _():
        signal(device_of(cores, plane - 1, me))

    @pl.when(plane < planes - 1)
    def _():
        signal(device_of(cores, plane + 1, me))

    peers = WB - 1 + jnp.minimum(plane, 1) + jnp.minimum(planes - 1 - plane, 1)
    pl.semaphore_wait(barrier, peers)


def cols(index, width):
    return pl.ds(pl.multiple_of(index * width, width), width)


def rows(index, base=0):
    return pl.ds(pl.multiple_of(base + index * BLOCK, BLOCK), BLOCK)


def stack(x):
    return jnp.concatenate([x[:, :HEAD], x[:, HEAD:]], axis=0)


def score_terms(q, g, kb, vb):
    s = lax.dot_general(kb, q, NT, preferred_element_type=jnp.float32)
    dp = lax.dot_general(vb, g, NT, preferred_element_type=jnp.float32)
    return s, dp


def soft_terms(s, dp, seen):
    tiles = []
    for i in range(WB + 1):
        tile = s[i * BLOCK : (i + 1) * BLOCK]
        if i < WB:
            tile = jnp.where(WB + 1 - i <= seen, tile, HIDDEN)
        else:
            kpos = lax.broadcasted_iota(jnp.int32, tile.shape, 0)
            qpos = lax.broadcasted_iota(jnp.int32, tile.shape, 1) % BLOCK
            tile = jnp.where(kpos <= qpos, tile, HIDDEN)
        tiles.append(tile)
    s = jnp.concatenate(tiles, axis=0)
    top = jnp.max(s, axis=0, keepdims=True)
    e = jnp.exp2((s - top) * (SCALE * LOG2E))
    inverse = 1.0 / jnp.sum(e, axis=0, keepdims=True)
    delta = jnp.sum(e * dp, axis=0, keepdims=True) * inverse
    p = e * inverse
    return p.astype(jnp.bfloat16), (p * (dp - delta)).astype(jnp.bfloat16)


def grad_terms(pb, ds, q, g, kb):
    dv = jnp.dot(pb, g, preferred_element_type=jnp.float32)
    dk = jnp.dot(ds, q, preferred_element_type=jnp.float32)
    dq = lax.dot_general(kb, ds, TN, preferred_element_type=jnp.float32)
    dq = (dq * SCALE).T.astype(jnp.bfloat16)
    return jnp.concatenate([dq[:BLOCK], dq[BLOCK:]], axis=1), dk, dv


def window_kernel(
    cores, planes, docs, band, q, k, v, g, oq, ok, ov,
    qh, gh, kw, vw, dk, dv, dq, part_k, part_v, back_k, back_v, sum_k, sum_v,
    gsend, grecv, zsend, zrecv, bsend, brecv, qsend, qrecv, rsend, rrecv,
):
    plane, me = place(cores)
    odd = (me // cores) % 2
    first, last = plane == 0, plane == planes - 1
    sources = ((k, kw, HEAD, WINDOW), (v, vw, HEAD, WINDOW), (q, qh, QW, 0), (g, gh, QW, 0))
    partial = ((dk, part_k, back_k, sum_k, ok), (dv, part_v, back_v, sum_v, ov))

    def remote(src, dst, send, recv, where):
        return pltpu.make_async_remote_copy(
            src_ref=src, dst_ref=dst, send_sem=send, recv_sem=recv,
            device_id=where, device_id_type=MESH,
        )

    def landed(ref, sem):
        pltpu.make_async_copy(ref, ref, sem).wait()

    def exchange(n, to):
        src, dst, w, base = sources[n]
        return remote(
            src.at[:, cols(to, w)], dst.at[rows(me, base), :], gsend.at[n, to], grecv.at[n, me],
            device_of(cores, plane, to),
        )

    def forward(n, of):
        dst = sources[n][1]
        return remote(
            dst.at[rows(of, WINDOW), :], dst.at[rows(of), :], zsend.at[n, of], zrecv.at[n, of],
            device_of(cores, plane + 1, me),
        )

    def backward(n, of):
        _, part, back, _, _ = partial[n]
        return remote(
            part.at[rows(of), :], back.at[rows(of), :], bsend.at[n, of], brecv.at[n, of],
            device_of(cores, plane - 1, me),
        )

    def give(src, out, w, to, send, recv):
        source, target = src.at[rows(to), :], out.at[:, cols(me, w)]

        @pl.when(to != me)
        def _():
            remote(source, target, send, recv, device_of(cores, plane, to)).start()

        @pl.when(to == me)
        def _():
            pltpu.make_async_copy(source, target, recv).start()

    def turn(i):
        return i + odd * (2 - 4 * ((i // 2) % 2))

    for n, (src, dst, w, base) in enumerate(sources):
        own = pltpu.make_async_copy(src.at[:, cols(me, w)], dst.at[rows(me, base), :], grecv.at[n, me])
        own.start()
    greet(cores, planes, plane, me)
    order = (3, 5, 4, 2, 6, 1, 7)
    for n in (0, 1):
        for r in order:
            exchange(n, (me + r) % WB).start()
    for r in order:
        for n in (2, 3):
            exchange(n, (me + r) % WB).start()

    dk[...] = jnp.zeros_like(dk)
    dv[...] = jnp.zeros_like(dv)

    @pl.when(first)
    def _():
        kw[pl.ds(0, WINDOW), :] = jnp.zeros((WINDOW, HEAD), kw.dtype)
        vw[pl.ds(0, WINDOW), :] = jnp.zeros((WINDOW, HEAD), vw.dtype)

    for n in (0, 1):
        for r in (0, 1, 7, 2, 6, 4, 3, 5):
            of = (me + r) % WB
            landed(sources[n][1].at[rows(of, WINDOW), :], grecv.at[n, of])

            @pl.when(jnp.logical_not(last))
            def _():
                forward(n, of).start()

    @pl.when(jnp.logical_not(first))
    def _():
        for n in (0, 1):

            @pl.loop(0, WB)
            def _(of):
                landed(sources[n][1].at[rows(of), :], zrecv.at[n, of])

    def send_back(j):
        @pl.when(jnp.logical_not(first))
        def _():
            part_k[rows(j), :] = (dk[rows(j), :] * SCALE).astype(jnp.bfloat16)
            part_v[rows(j), :] = dv[rows(j), :].astype(jnp.bfloat16)
            backward(0, j).start()
            backward(1, j).start()

    def seen_by(t):
        block = plane * WB + t
        seen = jnp.int32(0)
        for d in range(WB + 1):
            at = jnp.maximum(block - d, 0)
            visible = (d <= band[block]) & (block >= d) & (docs[at] == docs[block])
            seen = seen + visible.astype(jnp.int32)
        return seen

    def load(t):
        span = pl.ds(pl.multiple_of(t * BLOCK, BLOCK), SPAN)
        return stack(qh[rows(t), :]), stack(gh[rows(t), :]), kw[span, :], vw[span, :]

    def store(t, out, key_term, value_term):
        span = pl.ds(pl.multiple_of(t * BLOCK, BLOCK), SPAN)
        dk[span, :] += key_term
        dv[span, :] += value_term
        dq[rows(t), :] = out

    @pl.loop(0, WB // 2)
    def _(i):
        one = turn(2 * i)
        two = one + 1
        for t in (one, two):
            landed(qh.at[rows(t), :], grecv.at[2, t])
            landed(gh.at[rows(t), :], grecv.at[3, t])
        seen_one, seen_two = seen_by(one), seen_by(two)
        q1, g1, k1, v1 = load(one)
        q2, g2, k2, v2 = load(two)
        s1, dp1 = score_terms(q1, g1, k1, v1)
        s2, dp2 = score_terms(q2, g2, k2, v2)
        pb1, ds1 = soft_terms(s1, dp1, seen_one)
        store(one, *grad_terms(pb1, ds1, q1, g1, k1))
        pb2, ds2 = soft_terms(s2, dp2, seen_two)
        store(two, *grad_terms(pb2, ds2, q2, g2, k2))

        @pl.when(odd == 0)
        def _():
            send_back(one)
            send_back(two)

        @pl.when((odd == 1) & (i % 2 == 1))
        def _():
            for back in (2, 3, 0, 1):
                send_back(2 * i - 2 + back)

        for t in (one, two):
            give(dq, oq, QW, t, qsend.at[t], qrecv.at[me])

    @pl.loop(0, WB)
    def _(i):
        j = turn(i)
        for n in (0, 1):
            acc, _, back, total, out = partial[n]
            factor = SCALE if n == 0 else 1.0

            @pl.when(jnp.logical_not(last))
            def _():
                landed(back.at[rows(j), :], brecv.at[n, j])
                both = acc[rows(j, WINDOW), :] * factor + back[rows(j), :].astype(jnp.float32)
                total[rows(j), :] = both.astype(jnp.bfloat16)

            @pl.when(last)
            def _():
                total[rows(j), :] = (acc[rows(j, WINDOW), :] * factor).astype(jnp.bfloat16)

        for n in (0, 1):
            _, _, _, total, out = partial[n]
            give(total, out, HEAD, j, rsend.at[n, j], rrecv.at[n, me])

    @pl.loop(0, WB)
    def _(s):
        landed(oq.at[:, cols(s, QW)], qrecv.at[s])
        landed(ok.at[:, cols(s, HEAD)], rrecv.at[0, s])
        landed(ov.at[:, cols(s, HEAD)], rrecv.at[1, s])

        @pl.when(s != me)
        def _():
            for n in range(4):
                exchange(n, s).wait_send()
            where = device_of(cores, plane, s)
            remote(dq.at[rows(s), :], oq.at[:, cols(me, QW)], qsend.at[s], qrecv.at[me], where).wait_send()
            for n in (0, 1):
                _, _, _, total, out = partial[n]
                remote(
                    total.at[rows(s), :], out.at[:, cols(me, HEAD)], rsend.at[n, s], rrecv.at[n, me], where
                ).wait_send()

        for n in (0, 1):

            @pl.when(jnp.logical_not(last))
            def _():
                forward(n, s).wait_send()

            @pl.when(jnp.logical_not(first))
            def _():
                backward(n, s).wait_send()


def window_attention(cores, planes, docs, band, queries, keys, values, upstream):
    hbm = pl.BlockSpec(memory_space=pl.ANY)
    smem = pl.BlockSpec(memory_space=pltpu.SMEM)
    bf16, f32 = jnp.bfloat16, jnp.float32
    dma = pltpu.SemaphoreType.DMA
    return pl.pallas_call(
        functools.partial(window_kernel, cores, planes),
        out_shape=(
            jax.ShapeDtypeStruct((BLOCK, WB * QW), bf16),
            jax.ShapeDtypeStruct((BLOCK, WB * HEAD), bf16),
            jax.ShapeDtypeStruct((BLOCK, WB * HEAD), bf16),
        ),
        in_specs=[smem] * 2 + [hbm] * 4,
        out_specs=(hbm,) * 3,
        scratch_shapes=[pltpu.VMEM((WINDOW, QW), bf16)] * 2
        + [pltpu.VMEM((2 * WINDOW, HEAD), bf16)] * 2
        + [pltpu.VMEM((2 * WINDOW, HEAD), f32)] * 2
        + [pltpu.VMEM((WINDOW, QW), bf16)]
        + [pltpu.VMEM((WINDOW, HEAD), bf16)] * 6
        + [dma((4, WB))] * 2
        + [dma((2, WB))] * 4
        + [dma((WB,))] * 2
        + [dma((2, WB))] * 2,
        compiler_params=pltpu.CompilerParams(collective_id=0, has_side_effects=True),
        name="window_attention",
    )(docs, band, queries, keys, values, upstream)


def settle_kernel(*refs):
    ins, outs, stages = refs[:3], refs[3:6], refs[6:9]
    isem, osem = refs[9:]
    come = [pltpu.make_async_copy(a, b, isem.at[n]) for n, (a, b) in enumerate(zip(ins, stages))]
    leave = [pltpu.make_async_copy(b, c, osem.at[n]) for n, (b, c) in enumerate(zip(stages, outs))]
    for copy in come:
        copy.start()
    for n in (1, 2, 0):
        come[n].wait()
        leave[n].start()
    for copy in leave:
        copy.wait()


def settle(*grads):
    hbm = pl.BlockSpec(memory_space=pl.ANY)
    shapes = tuple(jax.ShapeDtypeStruct(a.shape, a.dtype) for a in grads)
    dma = pltpu.SemaphoreType.DMA
    return pl.pallas_call(
        settle_kernel,
        out_shape=shapes,
        in_specs=[hbm] * 3,
        out_specs=(hbm,) * 3,
        scratch_shapes=[pltpu.VMEM(a.shape, a.dtype) for a in grads] + [dma((3,)), dma((3,))],
        name="settle",
    )(*grads)


def solution(mesh):
    cores = mesh.shape["heads"]
    planes = mesh.shape["blk"] * cores // WB

    def per_device(queries, keys, values, upstream, doc_ids, band):
        grads = window_attention(cores, planes, doc_ids, band, queries, keys, values, upstream)
        return settle(*grads)

    split = P(("groups", "blk", "heads"), None)
    return jax.shard_map(
        per_device,
        mesh=mesh,
        in_specs=(split,) * 4 + (P("groups"),) * 2,
        out_specs=(split,) * 3,
        check_vma=False,
    )
```

profile of v0, /device:TPU:21, one launch (start us, length us, event | category | flops | bytes accessed | tf_op | source)
XLA Modules:
  0.0 46.6 jit_solution(3025135958126968789)
XLA Ops:
  0.6 43.8 %window_attention.1 = (bf16[128,2048]{1,0:T(8,128)(2,1)}, bf16[128,1024]{1,0:T(8,128)(2,1)}, bf16[128,1024]{1,0:T(8,128)(2,1)}) custom-call(s32[32]{0:T(128)} %docs.1, s32[32]{0:T(128)} %band.1, bf16[128,2048]{1,0:T(8,128)(2,1)} %q.1, bf16[128,1024]{1,0:T(8,128)(2,1)} %k.1, bf16[128,1024]{1,0:T(8,128)(2,1)} %v.1, bf16[128,2048]{1,0:T(8,128)(2,1)} %g.1), custom_call_target="tpu_custom_call" | custom-call | tf_op jit(solution)/shard_map/window_attention/pallas_call | solution.py:307
  44.5 2.1 %settle.1 = (bf16[128,2048]{1,0:T(8,128)(2,1)}, bf16[128,1024]{1,0:T(8,128)(2,1)}, bf16[128,1024]{1,0:T(8,128)(2,1)}) custom-call(bf16[128,2048]{1,0:T(8,128)(2,1)} %get-tuple-element.6.refs_0_, bf16[128,1024]{1,0:T(8,128)(2,1)} %get-tuple-element.7.refs_1_, bf16[128,1024]{1,0:T(8,128)(2,1)} %get-tuple-element.8.refs_2_), custom_call_target="tpu_custom_call" | custom-call | tf_op jit(solution)/shard_map/settle/pallas_call | solution.py:348
where the time goes:
time: 46.8 us; the launch traced here: 46.6 us
  Pallas kernels  45.9 us (98%)
  between operations  0.64 us (1%)
    pallas_call x1, Pallas kernels, window_attention(): pl.pallas_call(functools.partial(window_kernel, cores, planes), out_shape...  43.8 us
    pallas_call x1, Pallas kernels, settle(): pl.pallas_call(settle_kernel, out_shape=shapes, in_specs=[hbm] * 3, out_s...  2.13 us

commit v1 on v0

--- a/solution.py
+++ b/solution.py
@@ -306,13 +306,9 @@
     dma = pltpu.SemaphoreType.DMA
     return pl.pallas_call(
         functools.partial(window_kernel, cores, planes),
-        out_shape=(
-            jax.ShapeDtypeStruct((BLOCK, WB * QW), bf16),
-            jax.ShapeDtypeStruct((BLOCK, WB * HEAD), bf16),
-            jax.ShapeDtypeStruct((BLOCK, WB * HEAD), bf16),
-        ),
+        out_shape=tuple(pltpu.VMEM(a.shape, bf16) for a in (queries, keys, values)),
         in_specs=[smem] * 2 + [hbm] * 4,
-        out_specs=(hbm,) * 3,
+        out_specs=(pl.BlockSpec(memory_space=pltpu.VMEM),) * 3,
         scratch_shapes=[pltpu.VMEM((WINDOW, QW), bf16)] * 2
         + [pltpu.VMEM((2 * WINDOW, HEAD), bf16)] * 2
         + [pltpu.VMEM((2 * WINDOW, HEAD), f32)] * 2
@@ -328,31 +324,23 @@
 
 
 def settle_kernel(*refs):
-    ins, outs, stages = refs[:3], refs[3:6], refs[6:9]
-    isem, osem = refs[9:]
-    come = [pltpu.make_async_copy(a, b, isem.at[n]) for n, (a, b) in enumerate(zip(ins, stages))]
-    leave = [pltpu.make_async_copy(b, c, osem.at[n]) for n, (b, c) in enumerate(zip(stages, outs))]
-    for copy in come:
+    ins, outs, sems = refs[:3], refs[3:6], refs[6]
+    copies = [pltpu.make_async_copy(a, b, sems.at[n]) for n, (a, b) in enumerate(zip(ins, outs))]
+    for copy in copies:
         copy.start()
-    for n in (1, 2, 0):
-        come[n].wait()
-        leave[n].start()
-    for copy in leave:
+    for copy in copies:
         copy.wait()
 
 
 def settle(*grads):
-    hbm = pl.BlockSpec(memory_space=pl.ANY)
-    shapes = tuple(jax.ShapeDtypeStruct(a.shape, a.dtype) for a in grads)
-    dma = pltpu.SemaphoreType.DMA
     return pl.pallas_call(
         settle_kernel,
-        out_shape=shapes,
-        in_specs=[hbm] * 3,
-        out_specs=(hbm,) * 3,
-        scratch_shapes=[pltpu.VMEM(a.shape, a.dtype) for a in grads] + [dma((3,)), dma((3,))],
+        out_shape=tuple(jax.ShapeDtypeStruct(a.shape, a.dtype) for a in grads),
+        in_specs=[pl.BlockSpec(memory_space=pltpu.VMEM)] * 3,
+        out_specs=(pl.BlockSpec(memory_space=pl.ANY),) * 3,
+        scratch_shapes=[pltpu.SemaphoreType.DMA((3,))],
         name="settle",
-    )(*grads)
+    )(*(pltpu.with_memory_space_constraint(a, pltpu.VMEM) for a in grads))
 
 
 def solution(mesh):

time: 46.8 us -> 45.5 us (0.972)
  Pallas kernels: 45.9 us -> 44.7 us
    pallas_call x1, Pallas kernels: 2.13 us -> 0.99 us  [settle(): pl.pallas_call(settle_kernel, out_shape=tuple((jax.ShapeDtypeStruct(a.sha...]
where the time goes in v1:
time: 45.5 us; the launch traced here: 45.3 us
  Pallas kernels  44.7 us (98%)
  between operations  0.64 us (1%)
    pallas_call x1, Pallas kernels, window_attention(): pl.pallas_call(functools.partial(window_kernel, cores, planes), out_shape...  43.7 us
    pallas_call x1, Pallas kernels, settle(): pl.pallas_call(settle_kernel, out_shape=tuple((jax.ShapeDtypeStruct(a.sha...  0.99 us

profile of v1, /device:TPU:21, one launch (start us, length us, event | category | flops | bytes accessed | tf_op | source)
XLA Modules:
  0.0 45.3 jit_solution(7225652760126516689)
XLA Ops:
  0.6 43.7 %window_attention.1 = (bf16[128,2048]{1,0:T(8,128)(2,1)S(1)}, bf16[128,1024]{1,0:T(8,128)(2,1)S(1)}, bf16[128,1024]{1,0:T(8,128)(2,1)S(1)}) custom-call(s32[32]{0:T(128)} %docs.1, s32[32]{0:T(128)} %band.1, bf16[128,2048]{1,0:T(8,128)(2,1)} %q.1, bf16[128,1024]{1,0:T(8,128)(2,1)} %k.1, bf16[128,1024]{1,0:T(8,128)(2,1)} %v.1, bf16[128,2048]{1,0:T(8,128)(2,1)} %g.1), custom_call_target="tpu_custom_call" | custom-call | tf_op jit(solution)/shard_map/window_attention/pallas_call | solution.py:307
  44.3 1.0 %settle.1 = (bf16[128,2048]{1,0:T(8,128)(2,1)}, bf16[128,1024]{1,0:T(8,128)(2,1)}, bf16[128,1024]{1,0:T(8,128)(2,1)}) custom-call(bf16[128,2048]{1,0:T(8,128)(2,1)S(1)} %get-tuple-element.6.refs_0_, bf16[128,1024]{1,0:T(8,128)(2,1)S(1)} %get-tuple-element.7.refs_1_, bf16[128,1024]{1,0:T(8,128)(2,1)S(1)} %get-tuple-element.8.refs_2_), custom_call_target="tpu_custom_call" | custom-call | tf_op jit(solution)/shard_map/settle/pallas_call | solution.py:336

commit v2 on v1

--- a/solution.py
+++ b/solution.py
@@ -106,7 +106,6 @@
     gsend, grecv, zsend, zrecv, bsend, brecv, qsend, qrecv, rsend, rrecv,
 ):
     plane, me = place(cores)
-    odd = (me // cores) % 2
     first, last = plane == 0, plane == planes - 1
     sources = ((k, kw, HEAD, WINDOW), (v, vw, HEAD, WINDOW), (q, qh, QW, 0), (g, gh, QW, 0))
     partial = ((dk, part_k, back_k, sum_k, ok), (dv, part_v, back_v, sum_v, ov))
@@ -152,20 +151,22 @@
         def _():
             pltpu.make_async_copy(source, target, recv).start()
 
-    def turn(i):
-        return i + odd * (2 - 4 * ((i // 2) % 2))
-
     for n, (src, dst, w, base) in enumerate(sources):
         own = pltpu.make_async_copy(src.at[:, cols(me, w)], dst.at[rows(me, base), :], grecv.at[n, me])
         own.start()
     greet(cores, planes, plane, me)
-    order = (3, 5, 4, 2, 6, 1, 7)
-    for n in (0, 1):
-        for r in order:
-            exchange(n, (me + r) % WB).start()
-    for r in order:
+    chip, core = me // 2, me % 2
+    wide, tall, far = chip + 1 - 2 * (chip % 2), (chip + 2) % 4, 3 - chip
+    x0, x1 = 2 * wide + core, 2 * wide + 1 - core
+    y0, y1 = 2 * tall + core, 2 * tall + 1 - core
+    d0, d1 = 2 * far + core, 2 * far + 1 - core
+    beside = 2 * chip + 1 - core
+    for to in (beside, x0, y0, x1, y1, d0, d1):
+        for n in (0, 1):
+            exchange(n, to).start()
+    for to in (beside, y0, x0, y1, x1, d0, d1):
         for n in (2, 3):
-            exchange(n, (me + r) % WB).start()
+            exchange(n, to).start()
 
     dk[...] = jnp.zeros_like(dk)
     dv[...] = jnp.zeros_like(dv)
@@ -175,9 +176,8 @@
         kw[pl.ds(0, WINDOW), :] = jnp.zeros((WINDOW, HEAD), kw.dtype)
         vw[pl.ds(0, WINDOW), :] = jnp.zeros((WINDOW, HEAD), vw.dtype)
 
-    for n in (0, 1):
-        for r in (0, 1, 7, 2, 6, 4, 3, 5):
-            of = (me + r) % WB
+    for of in (me, beside, x0, y0, x1, y1, d0, d1):
+        for n in (0, 1):
             landed(sources[n][1].at[rows(of, WINDOW), :], grecv.at[n, of])
 
             @pl.when(jnp.logical_not(last))
@@ -219,9 +219,24 @@
         dv[span, :] += value_term
         dq[rows(t), :] = out
 
+    upper = chip // 2
+    near_first = (chip, 1 - chip, chip + 2, 3 - chip)
+    own_first = (chip, chip - 2, 3 - chip, 5 - chip)
+    order = [a + upper * (b - a) for a, b in zip(near_first, own_first)]
+
+    def visit(i):
+        return sum((i == n).astype(jnp.int32) * order[n] for n in range(4))
+
+    due = []
+    latest = jnp.int32(0)
+    for p in range(4):
+        when = sum(i * (order[i] == p).astype(jnp.int32) for i in range(4))
+        latest = jnp.maximum(latest, when)
+        due.append(latest)
+
     @pl.loop(0, WB // 2)
     def _(i):
-        one = turn(2 * i)
+        one = 2 * visit(i)
         two = one + 1
         for t in (one, two):
             landed(qh.at[rows(t), :], grecv.at[2, t])
@@ -236,22 +251,18 @@
         pb2, ds2 = soft_terms(s2, dp2, seen_two)
         store(two, *grad_terms(pb2, ds2, q2, g2, k2))
 
-        @pl.when(odd == 0)
-        def _():
-            send_back(one)
-            send_back(two)
-
-        @pl.when((odd == 1) & (i % 2 == 1))
-        def _():
-            for back in (2, 3, 0, 1):
-                send_back(2 * i - 2 + back)
+        for p in range(4):
+
+            @pl.when(i == due[p])
+            def _():
+                send_back(jnp.int32(2 * p))
+                send_back(jnp.int32(2 * p + 1))
 
         for t in (one, two):
             give(dq, oq, QW, t, qsend.at[t], qrecv.at[me])
 
     @pl.loop(0, WB)
-    def _(i):
-        j = turn(i)
+    def _(j):
         for n in (0, 1):
             acc, _, back, total, out = partial[n]
             factor = SCALE if n == 0 else 1.0

time: 45.5 us -> 42.5 us (0.934)
  Pallas kernels: 44.7 us -> 41.5 us
    pallas_call x1, Pallas kernels: 43.7 us -> 40.5 us  [window_attention(): pl.pallas_call(functools.partial(window_kernel, cores, planes), out_shape...]
where the time goes in v2:
time: 42.5 us; the launch traced here: 42.1 us
  Pallas kernels  41.5 us (98%)
  between operations  0.64 us (2%)
    pallas_call x1, Pallas kernels, window_attention(): pl.pallas_call(functools.partial(window_kernel, cores, planes), out_shape...  40.5 us
    pallas_call x1, Pallas kernels, settle(): pl.pallas_call(settle_kernel, out_shape=tuple((jax.ShapeDtypeStruct(a.sha...  0.99 us

profile of v2, /device:TPU:21, one launch (start us, length us, event | category | flops | bytes accessed | tf_op | source)
XLA Modules:
  0.0 42.1 jit_solution(781140022423403882)
XLA Ops:
  0.6 40.5 %window_attention.1 = (bf16[128,2048]{1,0:T(8,128)(2,1)S(1)}, bf16[128,1024]{1,0:T(8,128)(2,1)S(1)}, bf16[128,1024]{1,0:T(8,128)(2,1)S(1)}) custom-call(s32[32]{0:T(128)} %docs.1, s32[32]{0:T(128)} %band.1, bf16[128,2048]{1,0:T(8,128)(2,1)} %q.1, bf16[128,1024]{1,0:T(8,128)(2,1)} %k.1, bf16[128,1024]{1,0:T(8,128)(2,1)} %v.1, bf16[128,2048]{1,0:T(8,128)(2,1)} %g.1), custom_call_target="tpu_custom_call" | custom-call | tf_op jit(solution)/shard_map/window_attention/pallas_call | solution.py:318
  41.2 1.0 %settle.1 = (bf16[128,2048]{1,0:T(8,128)(2,1)}, bf16[128,1024]{1,0:T(8,128)(2,1)}, bf16[128,1024]{1,0:T(8,128)(2,1)}) custom-call(bf16[128,2048]{1,0:T(8,128)(2,1)S(1)} %get-tuple-element.6.refs_0_, bf16[128,1024]{1,0:T(8,128)(2,1)S(1)} %get-tuple-element.7.refs_1_, bf16[128,1024]{1,0:T(8,128)(2,1)S(1)} %get-tuple-element.8.refs_2_), custom_call_target="tpu_custom_call" | custom-call | tf_op jit(solution)/shard_map/settle/pallas_call | solution.py:347
